TPU v7x, 32 devices: a whole 2x2x4 slice. The times are simulated.
32 devices in a mesh: pix: 4 (over z), mode: 8 (over y, x, core).
Axes of the slice: x: 2, y: 2, z: 4, core: 2. Of those that a mesh axis runs over, the one named last changes fastest.
Arguments:
- frames: float32 [4, 4096, 8192], P(None, 'pix', 'mode'), may hold values from 0 to 500, as said below
- phase_steps: int32 [4], replicated, may hold values from 0 to 3, each once
- pattern_rows: int32 [8192], replicated, may hold values from 0 to 8191, each once
- probes: float32 [2, 32, 8192], replicated, may hold values from -6 to 6
Outputs:
- channels: float32 [2, 32, 8192], replicated
- fields: float32 [2, 32, 4096], P(None, None, ('pix', 'mode'))
- strengths: float32 [32], replicated
Inputs may be any that keep to these rules, and one draw needn't show every extreme that they name: `phase_steps`: each frame has its own phase step. `pattern_rows`: every Hadamard row is displayed exactly once. `frames`: intensities are not negative.
All inputs are finite; a program needn't handle non-finite values.
Results may differ from a plain program's by a relative error of at most 0.0003.
Values sent between devices are 32-bit elements; how exact they have to be, the bound alone decides.
No kernel may reach another device: no remote copies, remote signals or barrier semaphores. Data moves between devices by JAX's collectives and lax.ppermute only.
A program may use at most 128 MiB of HBM per device.

v0:
```python
import math
import jax
import jax.numpy as jnp
from jax import lax
from jax.sharding import PartitionSpec as P

HB = 128
ITERS = 2
precise = lax.Precision.HIGHEST


def demodulate(frames, phase_steps):
    cosine = (phase_steps == 0).astype(jnp.float32) - (phase_steps == 2).astype(jnp.float32)
    sine_part = (phase_steps == 1).astype(jnp.float32) - (phase_steps == 3).astype(jnp.float32)
    real_part = cosine[0] * frames[0]
    imag_part = sine_part[0] * frames[0]
    for frame_index in range(1, frames.shape[0]):
        real_part = real_part + cosine[frame_index] * frames[frame_index]
        imag_part = imag_part + sine_part[frame_index] * frames[frame_index]
    return (0.25 * real_part, 0.25 * imag_part)


def sign_table(table_order):
    positions = jnp.arange(table_order, dtype=jnp.int32)
    common = positions[:, None] & positions[None, :]
    parity = jnp.zeros((table_order, table_order), jnp.int32)
    for bit_place in range(table_order.bit_length() - 1):
        parity = parity + (common >> bit_place & 1)
    return (1 - 2 * (parity & 1)).astype(jnp.float32)


def hadamard_rows(values):
    length = values.shape[-1]
    leading = values.shape[:-1]
    inner_signs = sign_table(HB)
    outer_signs = sign_table(length // HB)
    shaped = values.reshape((-1, length // HB, HB))
    shaped = jnp.matmul(shaped, inner_signs, precision=precise)
    shaped = jnp.einsum("ab,nbc->nac", outer_signs, shaped, precision=precise)
    return shaped.reshape(leading + (length,)) * (1.0 / math.sqrt(length))


def contract_last(first_arg, second_arg):
    return lax.dot_general(first_arg, second_arg, (((1,), (1,)), ((), ())), precision=precise)


def forward(matrix, vectors):
    real_out = contract_last(vectors[0], matrix[0]) - contract_last(vectors[1], matrix[1])
    imag_out = contract_last(vectors[1], matrix[0]) + contract_last(vectors[0], matrix[1])
    return jnp.stack([real_out, imag_out])


def backward(matrix, images):
    real_out = jnp.dot(images[0], matrix[0], precision=precise) + jnp.dot(
        images[1], matrix[1], precision=precise
    )
    imag_out = jnp.dot(images[1], matrix[0], precision=precise) - jnp.dot(
        images[0], matrix[1], precision=precise
    )
    return jnp.stack([real_out, imag_out])


def orthonormal(vectors):
    mode_count = vectors.shape[2]
    stacked = jnp.concatenate([vectors[0], vectors[1]], axis=1)
    gram_matrix = jnp.dot(stacked, stacked.T, precision=precise)
    factor = jnp.linalg.cholesky(gram_matrix)
    solved = lax.linalg.triangular_solve(factor, stacked, left_side=True, lower=True)
    return jnp.stack([solved[:, :mode_count], solved[:, mode_count:]])


def local(frames, phase_steps, pattern_rows, probes):
    columns = frames.shape[2]
    groups = lax.axis_size("mode")
    modes_total = columns * groups
    devices = lax.axis_size("pix") * groups
    real_part, imag_part = demodulate(frames, phase_steps)
    positions = jnp.arange(modes_total, dtype=jnp.int32)
    inverse = jnp.zeros((modes_total,), jnp.int32).at[pattern_rows].set(positions)
    current = orthonormal(probes)
    rows_here = real_part.shape[0] // groups
    demodulated = jnp.stack([real_part, imag_part]).reshape(2, groups, rows_here, columns)
    ordered = jnp.take(
        lax.all_to_all(demodulated, "mode", split_axis=1, concat_axis=3, tiled=True),
        inverse,
        axis=3,
    )
    matrix = hadamard_rows(ordered)
    matrix = matrix.reshape(2, rows_here, modes_total)
    for iteration in range(ITERS):
        images = forward(matrix, current)
        returned = lax.psum(backward(matrix, images), ("pix", "mode"))
        current = orthonormal(returned)
    fields = forward(matrix, current)
    local_power = jnp.sum(fields * fields, axis=(0, 2))
    strengths = lax.psum(local_power, ("pix", "mode")) / (fields.shape[2] * devices)
    channels = math.sqrt(modes_total) * current
    return (channels, fields, strengths)


def solution(mesh):
    in_specs = (P(None, "pix", "mode"), P(), P(), P())
    out_specs = (P(), P(None, None, ("pix", "mode")), P())
    return jax.shard_map(local, mesh=mesh, in_specs=in_specs, out_specs=out_specs, check_vma=False)
```

profile of v0, /device:TPU:0, one launch (start us, length us, event | category | flops | bytes accessed | tf_op | source)
XLA Modules:
  0.0 704.6 jit_solution(8088165573559418275)
XLA Ops:
  7.2 0.7 fusion.188
  7.8 0.7 fusion.211
  8.5 12.0 %add_multiply_fusion.1 = (f32[1,1024,1024]{2,1,0:T(8,128)S(1)}, f32[1,1024,1024]{2,1,0:T(8,128)S(1)}) fusion(f32[4,1024,1024]{2,1,0:T(8,128)} %param.7, f32[]{:T(128)} %bitcast.9, f32[]{:T(128)} %bitcast.8, f32[]{:T(128)} %bitcast.7, f32[]{:T(128)} %bitcast.6, f32[]{:T(128)} %bitcast.14, f32[]{:T(128)} %bitcast.13, f32[]{:T(128)} %bitcast.12, f32[]{:T(128)} %bitcast.11), kind=kLoop, calls=%fused_computation.52 | loop fusion | flops 16777216 | bytes 25165856 | tf_op jit(solution)/shard_map/mul | solution.py:20
  20.5 1.7 pad_maximum_fusion
  22.2 4.1 copy.21
  26.3 5.3 all-to-all-start
  31.8 1.0 copy-done.6
  32.8 1.8 fusion.69
  34.6 2.9 cholesky.59
  37.6 0.6 compare_reduce_fusion.2
  38.2 0.7 fusion.167
  38.9 2.4 custom-call.7
  41.4 30.7 %scatter_custom_fusion = s32[8192]{0:T(1024)S(1)} fusion(s32[8192]{0:T(1024)S(1)} %compare_select_fusion.1, s32[8192]{0:T(1024)S(1)} %iota.46, s32[]{:T(128)} %constant.66.clone.1), kind=kCustom, calls=%fused_computation.208 | custom fusion | bytes 32772 | tf_op jit(solution)/shard_map/scatter | solution.py:79
  72.1 3.1 fusion.68
  75.2 50.9 %all-to-all-done = f32[2,8,128,1024]{3,2,0,1:T(8,128)} async-done(((f32[2,8,128,1024]{3,2,0,1:T(8,128)}), f32[2,8,128,1024]{3,2,0,1:T(8,128)}, u32[]{:S(2)}, u32[]{:S(2)}) %all-to-all-start) | async-done | bytes 8388640 | tf_op jit(solution)/shard_map/all_to_all | solution.py:84
  126.1 8.7 %copy.22 = f32[2,8,128,1024]{2,3,1,0:T(8,128)} copy(f32[2,8,128,1024]{3,2,0,1:T(8,128)} %all-to-all-done) | data formatting | bytes 16777216 | tf_op jit(solution)/shard_map/all_to_all | solution.py:84
  134.8 15.4 %copy.23 = f32[2,128,8192]{1,0,2:T(2,128)} copy(f32[2,128,8192]{1,2,0:T(8,128)} %bitcast.173) | data formatting | bytes 16777216 | tf_op jit(solution)/shard_map/all_to_all | solution.py:84
  150.1 59.4 %gather_fusion = f32[8192,2,128]{2,1,0:T(2,128)} fusion(f32[2,128,8192]{1,0,2:T(2,128)} %copy.23, s32[8192]{0:T(1024)S(1)} %fusion.166), kind=kCustom, calls=%fused_computation | custom fusion | bytes 16809984 | tf_op jit(solution)/shard_map/jit(_take)/gather | solution.py:83
  209.5 11.5 %gather.7 = f32[256,64,128]{0,2,1:T(8,128)} reshape(f32[2,128,8192]{1,0,2:T(2,128)} %bitcast.172) | data formatting | bytes 16777216 | tf_op jit(solution)/shard_map/jit(_take)/gather | solution.py:83
  221.0 8.7 %copy.24 = f32[256,64,128]{2,1,0:T(8,128)} copy(f32[256,64,128]{0,2,1:T(8,128)} %gather.7) | data formatting | bytes 16777216 | tf_op jit(solution)/shard_map/jit(_take)/gather | solution.py:83
  229.7 13.0 %fusion.4 = f32[256,64,128]{2,1,0:T(8,128)S(1)} fusion(f32[256,64,128]{2,1,0:T(8,128)} %copy.24, pred[64,128]{1,0:T(8,128)(4,1)S(1)} %and_bitcast_fusion), kind=kOutput, calls=%fused_computation.12 | convolution fusion | flops 3223732224 | bytes 16785408 | tf_op jit(solution)/shard_map/dot_general | solution.py:38
  242.8 8.9 %multiply_bitcast_fusion = f32[256,64,128]{2,1,0:T(8,128)S(1)} fusion(f32[256,64,128]{2,1,0:T(8,128)S(1)} %fusion.4), kind=kOutput, calls=%fused_computation.11 | convolution fusion | flops 1612800000 | bytes 16777216 | tf_op jit(solution)/shard_map/ab,nbc->nac/dot_general | solution.py:39
  251.6 1.7 fusion.210
  253.3 5.8 fusion.20
  259.1 5.6 fusion.18
  264.7 5.6 fusion.70
  270.3 4.8 fusion.38
  275.0 5.7 fusion.73
  280.7 4.9 fusion.34
  285.6 4.6 fusion.3
  290.2 4.6 fusion.2
  294.8 1.5 pad_maximum_fusion.2
  296.6 134.8 %all-reduce.3.cloned.1.call-done = f32[2,32,8192]{2,1,0:T(8,128)} async-done(((f32[2,32,8192]{2,1,0:T(8,128)}), f32[2,32,8192]{2,1,0:T(8,128)}) %all-reduce.3.cloned.1.call-update) | async-done | bytes 2097168 | tf_op jit(solution)/shard_map/psum | solution.py:92
  431.4 1.7 slice_bitcast_fusion.3
  433.1 1.8 fusion.67
  434.9 2.9 cholesky.70
  437.9 0.6 compare_reduce_fusion.1
  438.5 0.7 fusion.168
  439.2 2.4 custom-call.8
  441.6 1.9 fusion.66
  443.9 5.6 fusion.14
  449.4 5.8 fusion.12
  455.2 5.6 fusion.76
  460.8 4.5 fusion.30
  465.3 6.0 fusion.79
  471.4 4.5 fusion.26
  475.9 4.8 fusion.1
  480.7 4.6 fusion
  485.3 1.5 pad_maximum_fusion.4
  486.8 133.5 %all-reduce.5.cloned.1.call-done = f32[2,32,8192]{2,1,0:T(8,128)} async-done(((f32[2,32,8192]{2,1,0:T(8,128)}), f32[2,32,8192]{2,1,0:T(8,128)}) %all-reduce.5.cloned.1.call-update) | async-done | bytes 2097168 | tf_op jit(solution)/shard_map/psum | solution.py:92
  620.3 1.7 slice_bitcast_fusion.1
  622.0 1.8 fusion.65
  623.8 2.9 cholesky.81
  626.8 0.6 compare_reduce_fusion
  627.4 0.7 fusion.169
  628.1 2.4 custom-call.9
  630.5 1.9 fusion.64
  632.7 5.8 fusion.8
  638.5 5.6 fusion.6
  644.3 5.8 fusion.85
  650.1 5.6 fusion.91
  655.7 0.7 multiply_reduce_fusion
  656.4 38.9 %psum.23 = f32[32]{0:T(128)S(1)} all-reduce(f32[32]{0:T(128)S(1)} %get-tuple-element.5), channel_id=1, replica_groups=mesh['pix'=4,'mode'=8] {'pix','mode'}, use_global_device_ids=true, to_apply=%region_6.9 | all-reduce | flops 32 | bytes 256 | tf_op jit(solution)/shard_map/psum | solution.py:96
  695.9 1.5 maximum_multiply_fusion
  (37 shorter events, 2.1 us)
Async XLA Ops:
  26.3 5.4 copy-start.7
  26.3 99.8 %all-to-all-start = ((f32[2,8,128,1024]{3,2,0,1:T(8,128)}), f32[2,8,128,1024]{3,2,0,1:T(8,128)}, u32[]{:S(2)}, u32[]{:S(2)}) async-start(f32[2,8,128,1024]{3,2,0,1:T(8,128)} %copy.21), calls=%async_computation | async-start | bytes 16777216 | tf_op jit(solution)/shard_map/all_to_all | solution.py:84
  31.6 9.7 %copy-start.8 = (s32[8192]{0:T(1024)S(1)}, s32[8192]{0:T(1024)}, u32[]{:S(2)}) copy-start(s32[8192]{0:T(1024)} %param.9) | copy-start | bytes 98308
  31.6 399.8 %all-reduce.3.cloned.1.call-start = ((), (), s32[]{:S(2)}) async-start(), calls=%async_computation.1 | async-start | bytes 4194304 | tf_op jit(solution)/shard_map/psum | solution.py:92
  31.8 1.0 copy-start.6
  253.3 27.4 %copy-start = (f32[128,64,128]{2,1,0:T(8,128)}, f32[128,64,128]{2,1,0:T(8,128)S(1)}, u32[]{:S(2)}) copy-start(f32[128,64,128]{2,1,0:T(8,128)S(1)} %get-tuple-element.9) | copy-start | bytes 12582916
  253.3 36.9 %copy-start.3 = (f32[128,64,128]{2,1,0:T(8,128)}, f32[128,64,128]{2,1,0:T(8,128)S(1)}, u32[]{:S(2)}) copy-start(f32[128,64,128]{2,1,0:T(8,128)S(1)} %get-tuple-element.10) | copy-start | bytes 12582916
  296.4 323.9 %all-reduce.5.cloned.1.call-start = ((), (), s32[]{:S(2)}) async-start(), calls=%async_computation.2 | async-start | bytes 4194304 | tf_op jit(solution)/shard_map/psum | solution.py:92
  441.6 2.2 copy-start.4
  443.9 11.4 %copy-start.1 = (f32[128,64,128]{2,1,0:T(8,128)S(1)}, f32[128,64,128]{2,1,0:T(8,128)}, u32[]{:S(2)}) copy-start(f32[128,64,128]{2,1,0:T(8,128)} %copy-done) | copy-start | bytes 12582916
  630.5 2.2 copy-start.5
  638.5 5.7 copy-start.2
Sparse Core Ops, SparseCore 0:
  296.5 134.8 all-reduce.2
  486.9 133.3 all-reduce.4
where the time goes:
time: 711 us; the launch traced here: 705 us
  waiting for transfers between devices  319 us (45%)
  local copies, waits for them, and re-layouts  146 us (21%)
  matrix products  140 us (20%)
  other arithmetic  40.2 us (6%)
  blocking collectives  38.9 us (5%)
  between operations  14.9 us (2%)
    psum x2, waiting for transfers between devices, local(): returned = lax.psum(backward(matrix, images), ('pix', 'mode'))  268 us
    gather x3, local copies, waits for them, and re-layouts, local(): jnp.take(lax.all_to_all(demodulated, 'mode', split_axis=1, concat_axis=3,...  79.6 us
    dot_general x12, matrix products, contract_last(): lax.dot_general(first_arg, second_arg, (((1,), (1,)), ((), ())), precisio...  68.3 us
    all_to_all x1, waiting for transfers between devices, local(): lax.all_to_all(demodulated, 'mode', split_axis=1, concat_axis=3, tiled=True)  50.9 us
    psum x1, blocking collectives, local(): lax.psum(local_power, ('pix', 'mode')) / (fields.shape[2] * devices)  38.9 us
    scatter x1, local copies, waits for them, and re-layouts, local(): jnp.zeros((modes_total,), jnp.int32).at[pattern_rows].set(positions)  30.7 us
    all_to_all x2, local copies, waits for them, and re-layouts, local(): lax.all_to_all(demodulated, 'mode', split_axis=1, concat_axis=3, tiled=True)  24 us
  transfers between devices with their start and end apart: 3, of which 3 were waited for; matrix products, arithmetic and copies ran while one was open for 6% of the time, Pallas kernels for 0%

commit v1 on v0

--- a/solution.py
+++ b/solution.py
@@ -7,6 +7,22 @@
 HB = 128
 ITERS = 2
 precise = lax.Precision.HIGHEST
+
+
+def pairwise_exchange(array, axis, split, join):
+    ways, here = (lax.axis_size(axis), lax.axis_index(axis))
+    width = array.shape[split] // ways
+    dims = list(array.shape)
+    dims[split] = width
+    height = dims[join]
+    dims[join] = height * ways
+    full = jnp.zeros(dims, array.dtype)
+    for mask in range(ways):
+        part = lax.dynamic_slice_in_dim(array, (here ^ mask) * width, width, axis=split)
+        if mask:
+            part = lax.ppermute(part, axis, [(d, d ^ mask) for d in range(ways)])
+        full = lax.dynamic_update_slice_in_dim(full, part, (here ^ mask) * height, axis=join)
+    return full
 
 
 def demodulate(frames, phase_steps):
@@ -80,11 +96,7 @@
     current = orthonormal(probes)
     rows_here = real_part.shape[0] // groups
     demodulated = jnp.stack([real_part, imag_part]).reshape(2, groups, rows_here, columns)
-    ordered = jnp.take(
-        lax.all_to_all(demodulated, "mode", split_axis=1, concat_axis=3, tiled=True),
-        inverse,
-        axis=3,
-    )
+    ordered = jnp.take(pairwise_exchange(demodulated, "mode", 1, 3), inverse, axis=3)
     matrix = hadamard_rows(ordered)
     matrix = matrix.reshape(2, rows_here, modes_total)
     for iteration in range(ITERS):

time: 711 us -> 727 us (1.023)
  waiting for transfers between devices: 319 us -> 303 us
  local copies, waits for them, and re-layouts: 146 us -> 160 us
  other arithmetic: 40.2 us -> 53.9 us
    all_to_all x1 -> x0, waiting for transfers between devices: 50.9 us -> none  [local(): lax.all_to_all(demodulated, 'mode', split_axis=1, concat_axis=3, tiled=True)]
    ppermute x0 -> x7, waiting for transfers between devices: none -> 33.2 us  [pairwise_exchange(): part = lax.ppermute(part, axis, [(d, d ^ mask) for d in range(ways)])]
    all_to_all x2 -> x0, local copies, waits for them, and re-layouts: 24 us -> none  [local(): lax.all_to_all(demodulated, 'mode', split_axis=1, concat_axis=3, tiled=True)]
    dynamic_update_slice x0 -> x8, local copies, waits for them, and re-layouts: none -> 19 us  [pairwise_exchange(): lax.dynamic_update_slice_in_dim(full, part, (here ^ mask) * height, axis=...]
    another operation x1 -> x2, local copies, waits for them, and re-layouts: 4.06 us -> 21.8 us  [local(): jnp.stack([real_part, imag_part]).reshape(2, groups, rows_here, columns)]
    another operation x1 -> x2, other arithmetic: 1.65 us -> 11 us  [local(): jnp.stack([real_part, imag_part]).reshape(2, groups, rows_here, columns)]
    ppermute x0 -> x7, starting transfers between devices: none -> 7.69 us  [pairwise_exchange(): part = lax.ppermute(part, axis, [(d, d ^ mask) for d in range(ways)])]
  transfers between devices with their start and end apart: 3 -> 9, of which waited for: 3 -> 4; matrix products, arithmetic and copies ran while one was open for 6% -> 9% of each run, Pallas kernels for 0% -> 0%
where the time goes in v1:
time: 727 us; the launch traced here: 718 us
  waiting for transfers between devices  303 us (42%)
  local copies, waits for them, and re-layouts  160 us (22%)
  matrix products  140 us (19%)
  other arithmetic  53.9 us (7%)
  blocking collectives  38.9 us (5%)
  between operations  15 us (2%)
  starting transfers between devices  7.95 us (1%)
    psum x2, waiting for transfers between devices, local(): returned = lax.psum(backward(matrix, images), ('pix', 'mode'))  270 us
    gather x3, local copies, waits for them, and re-layouts, local(): jnp.take(pairwise_exchange(demodulated, 'mode', 1, 3), inverse, axis=3)  79.7 us
    dot_general x12, matrix products, contract_last(): lax.dot_general(first_arg, second_arg, (((1,), (1,)), ((), ())), precisio...  68.2 us
    psum x1, blocking collectives, local(): lax.psum(local_power, ('pix', 'mode')) / (fields.shape[2] * devices)  38.9 us
    ppermute x7, waiting for transfers between devices, pairwise_exchange(): part = lax.ppermute(part, axis, [(d, d ^ mask) for d in range(ways)])  33.2 us
    scatter x1, local copies, waits for them, and re-layouts, local(): jnp.zeros((modes_total,), jnp.int32).at[pattern_rows].set(positions)  30.7 us
    another operation x2, local copies, waits for them, and re-layouts, local(): jnp.stack([real_part, imag_part]).reshape(2, groups, rows_here, columns)  21.8 us
    dynamic_update_slice x8, local copies, waits for them, and re-layouts, pairwise_exchange(): lax.dynamic_update_slice_in_dim(full, part, (here ^ mask) * height, axis=...  19 us
  transfers between devices with their start and end apart: 9, of which 4 were waited for; matrix products, arithmetic and copies ran while one was open for 9% of the time, Pallas kernels for 0%

profile of v1, /device:TPU:0, one launch (start us, length us, event | category | flops | bytes accessed | tf_op | source)
XLA Modules:
  0.0 718.0 jit_solution(3694104323222999715)
XLA Ops:
  8.6 14.5 %add_multiply_fusion.1 = (f32[1,1024,1024]{2,1,0:T(8,128)}, f32[1,1024,1024]{2,1,0:T(8,128)}) fusion(f32[4,1024,1024]{2,1,0:T(8,128)} %param.7, f32[]{:T(128)} %bitcast.9, f32[]{:T(128)} %bitcast.8, f32[]{:T(128)} %bitcast.7, f32[]{:T(128)} %bitcast.6, f32[]{:T(128)} %bitcast.14, f32[]{:T(128)} %bitcast.13, f32[]{:T(128)} %bitcast.12, f32[]{:T(128)} %bitcast.11), kind=kLoop, calls=%fused_computation.67 | loop fusion | flops 16777216 | bytes 25165856 | tf_op jit(solution)/shard_map/mul | solution.py:36
  23.1 10.9 %copy.15 = f32[1,8,128,1024]{2,0,3,1:T(1,128)} copy(f32[1,8,128,1024]{3,2,1,0:T(8,128)} %bitcast.185) | data formatting | bytes 8388608 | tf_op jit(solution)/shard_map/stack | solution.py:98
  33.9 10.9 %copy.14 = f32[1,8,128,1024]{2,0,3,1:T(1,128)} copy(f32[1,8,128,1024]{3,2,1,0:T(8,128)} %bitcast.184) | data formatting | bytes 8388608 | tf_op jit(solution)/shard_map/stack | solution.py:98
  44.9 9.0 %fusion.94 = (f32[2,1,128,1024]{2,0,3,1:T(2,128)}, f32[2,1,128,1024]{2,0,3,1:T(2,128)}, f32[2,1,128,1024]{2,0,3,1:T(2,128)}, f32[2,1,128,1024]{2,0,3,1:T(2,128)}...) fusion(s32[]{:T(128)S(6)} %select_n.82, f32[1,8,128,1024]{2,0,3,1:T(1,128)} %copy.14, ...), kind=kLoop, calls=%fused_computation.109 | loop fusion | flops 1572864 | bytes 14680088 | tf_op jit(solution)/shard_map/stack | solution.py:98
  54.4 2.6 collective-permute-start.1
  57.0 1.8 collective-permute-start.3
  59.9 1.8 fusion.69
  61.8 2.9 cholesky.59
  66.1 5.4 broadcast.105
  72.4 1.9 bitcast_dynamic-update-slice_fusion.7
  74.4 2.0 fusion.101
  76.4 2.4 custom-call.7
  78.8 30.7 %scatter_custom_fusion = s32[8192]{0:T(1024)S(1)} fusion(s32[8192]{0:T(1024)S(1)} %compare_select_fusion.1, s32[8192]{0:T(1024)S(1)} %iota.46, s32[]{:T(128)} %constant.35.clone.1), kind=kCustom, calls=%fused_computation.239 | custom fusion | bytes 32772 | tf_op jit(solution)/shard_map/scatter | solution.py:95
  109.5 3.2 fusion.68
  112.8 2.7 collective-permute-start.5
  115.5 2.3 bitcast_dynamic-update-slice_fusion.6
  117.9 2.3 bitcast_dynamic-update-slice_fusion.5
  120.2 2.3 bitcast_dynamic-update-slice_fusion.4
  122.4 2.3 bitcast_dynamic-update-slice_fusion.3
  124.7 2.3 bitcast_dynamic-update-slice_fusion.2
  127.0 12.8 %collective-permute-done.5 = f32[2,1,128,1024]{2,0,3,1:T(2,128)S(1)} collective-permute-done((f32[2,1,128,1024]{2,0,3,1:T(2,128)S(1)}, f32[2,1,128,1024]{2,0,3,1:T(2,128)S(1)}, u32[]{:S(2)}, u32[]{:S(2)}) %collective-permute-start.5) | collective-permute-done | bytes 1048608 | tf_op jit(solution)/shard_map/ppermute | solution.py:23
  140.8 20.4 %collective-permute-done.6 = f32[2,1,128,1024]{2,0,3,1:T(2,128)S(1)} collective-permute-done((f32[2,1,128,1024]{2,0,3,1:T(2,128)}, f32[2,1,128,1024]{2,0,3,1:T(2,128)S(1)}, u32[]{:S(2)}, u32[]{:S(2)}) %collective-permute-start.6) | collective-permute-done | bytes 1048608 | tf_op jit(solution)/shard_map/ppermute | solution.py:23
  162.3 59.4 %gather_fusion = f32[8192,2,128]{2,1,0:T(2,128)} fusion(f32[2,128,8192]{1,0,2:T(2,128)} %bitcast_dynamic-update-slice_fusion, s32[8192]{0:T(1024)S(1)} %fusion.174), kind=kCustom, calls=%fused_computation | custom fusion | bytes 16809984 | tf_op jit(solution)/shard_map/jit(_take)/gather | solution.py:99
  221.7 11.5 %gather.7 = f32[256,64,128]{0,2,1:T(8,128)} reshape(f32[2,128,8192]{1,0,2:T(2,128)} %bitcast.183) | data formatting | bytes 16777216 | tf_op jit(solution)/shard_map/jit(_take)/gather | solution.py:99
  233.2 8.7 %copy.16 = f32[256,64,128]{2,1,0:T(8,128)} copy(f32[256,64,128]{0,2,1:T(8,128)} %gather.7) | data formatting | bytes 16777216 | tf_op jit(solution)/shard_map/jit(_take)/gather | solution.py:99
  242.0 13.0 %fusion.4 = f32[256,64,128]{2,1,0:T(8,128)S(1)} fusion(f32[256,64,128]{2,1,0:T(8,128)} %copy.16, pred[64,128]{1,0:T(8,128)(4,1)S(1)} %and_bitcast_fusion), kind=kOutput, calls=%fused_computation.27 | convolution fusion | flops 3223732224 | bytes 16785408 | tf_op jit(solution)/shard_map/dot_general | solution.py:54
  255.0 8.9 %multiply_bitcast_fusion = f32[256,64,128]{2,1,0:T(8,128)S(1)} fusion(f32[256,64,128]{2,1,0:T(8,128)S(1)} %fusion.4), kind=kOutput, calls=%fused_computation.26 | convolution fusion | flops 1612800000 | bytes 16777216 | tf_op jit(solution)/shard_map/ab,nbc->nac/dot_general | solution.py:55
  263.9 1.7 fusion.218
  265.5 5.8 fusion.18
  271.3 5.6 fusion.20
  276.9 5.6 fusion.73
  282.5 4.8 fusion.34
  287.3 5.6 fusion.70
  292.9 4.9 fusion.38
  297.9 4.6 fusion.2
  302.5 4.6 fusion.3
  307.0 1.5 pad_maximum_fusion.1
  308.8 136.1 %all-reduce.3.cloned.1.call-done = f32[2,32,8192]{2,1,0:T(8,128)} async-done(((f32[2,32,8192]{2,1,0:T(8,128)}), f32[2,32,8192]{2,1,0:T(8,128)}) %all-reduce.3.cloned.1.call-update) | async-done | bytes 2097168 | tf_op jit(solution)/shard_map/psum | solution.py:104
  444.9 1.7 slice_bitcast_fusion.3
  446.6 1.8 fusion.67
  448.4 2.9 cholesky.70
  452.7 2.4 custom-call.8
  455.1 1.9 fusion.66
  457.4 5.6 fusion.12
  462.9 5.8 fusion.14
  468.7 5.6 fusion.79
  474.3 4.5 fusion.26
  478.9 6.0 fusion.76
  484.9 4.5 fusion.30
  489.4 4.8 fusion
  494.2 4.6 fusion.1
  498.8 1.5 pad_maximum_fusion.3
  500.3 133.6 %all-reduce.5.cloned.1.call-done = f32[2,32,8192]{2,1,0:T(8,128)} async-done(((f32[2,32,8192]{2,1,0:T(8,128)}), f32[2,32,8192]{2,1,0:T(8,128)}) %all-reduce.5.cloned.1.call-update) | async-done | bytes 2097168 | tf_op jit(solution)/shard_map/psum | solution.py:104
  633.8 1.7 slice_bitcast_fusion.1
  635.5 1.8 fusion.65
  637.4 2.9 cholesky.81
  641.6 2.4 custom-call.9
  644.1 1.9 fusion.64
  646.3 5.8 fusion.6
  652.1 5.6 fusion.8
  657.6 5.9 fusion.91
  663.5 5.6 fusion.85
  669.8 38.9 %psum.23 = f32[32]{0:T(128)S(1)} all-reduce(f32[32]{0:T(128)S(1)} %get-tuple-element.5), channel_id=1, replica_groups=mesh['pix'=4,'mode'=8] {'pix','mode'}, use_global_device_ids=true, to_apply=%region_6.9 | all-reduce | flops 32 | bytes 256 | tf_op jit(solution)/shard_map/psum | solution.py:108
  709.2 1.5 maximum_multiply_fusion
  (64 shorter events, 12.6 us)
Async XLA Ops:
  7.2 437.7 %all-reduce.3.cloned.1.call-start = ((), (), s32[]{:S(2)}) async-start(), calls=%async_computation | async-start | bytes 4194304 | tf_op jit(solution)/shard_map/psum | solution.py:104
  44.9 13.9 %copy-start.11 = (s32[8192]{0:T(1024)S(1)}, s32[8192]{0:T(1024)}, u32[]{:S(2)}) copy-start(s32[8192]{0:T(1024)} %param.9) | copy-start | bytes 98308
  44.9 13.9 %copy-start.9 = (f32[2,32,8192]{2,1,0:T(8,128)S(1)}, f32[2,32,8192]{2,1,0:T(8,128)}, u32[]{:S(2)}) copy-start(f32[2,32,8192]{2,1,0:T(8,128)} %param.10) | copy-start | bytes 6291460
  53.9 58.9 %collective-permute-start = (f32[2,1,128,1024]{2,0,3,1:T(2,128)}, f32[2,1,128,1024]{2,0,3,1:T(2,128)}, u32[]{:S(2)}, u32[]{:S(2)}) collective-permute-start(f32[2,1,128,1024]{2,0,3,1:T(2,128)} %get-tuple-element.12), channel_id=1, source_target_pairs={{0,1},{1,0},{2,3},{3,2},{4,5},{5,4},{6,7},{7,6},{8,9},{9,8},{10,11... | collective-permute-start | bytes 3145736 | tf_op jit(solution)/shard_map/ppermute | solution.py:23
  54.4 63.4 %collective-permute-start.1 = (f32[2,1,128,1024]{2,0,3,1:T(2,128)}, f32[2,1,128,1024]{2,0,3,1:T(2,128)}, u32[]{:S(2)}, u32[]{:S(2)}) collective-permute-start(f32[2,1,128,1024]{2,0,3,1:T(2,128)} %get-tuple-element.13), channel_id=1, source_target_pairs={{0,2},{1,3},{2,0},{3,1},{4,6},{5,7},{6,4},{7,5},{8,10},{9,11},{10,... | collective-permute-start | bytes 3145736 | tf_op jit(solution)/shard_map/ppermute | solution.py:23
  57.0 63.2 %collective-permute-start.2 = (f32[2,1,128,1024]{2,0,3,1:T(2,128)}, f32[2,1,128,1024]{2,0,3,1:T(2,128)}, u32[]{:S(2)}, u32[]{:S(2)}) collective-permute-start(f32[2,1,128,1024]{2,0,3,1:T(2,128)} %get-tuple-element.14), channel_id=1, source_target_pairs={{0,3},{1,2},{2,1},{3,0},{4,7},{5,6},{6,5},{7,4},{8,11},{9,10},{10,... | collective-permute-start | bytes 3145736 | tf_op jit(solution)/shard_map/ppermute | solution.py:23
  57.0 65.4 %collective-permute-start.3 = (f32[2,1,128,1024]{2,0,3,1:T(2,128)}, f32[2,1,128,1024]{2,0,3,1:T(2,128)}, u32[]{:S(2)}, u32[]{:S(2)}) collective-permute-start(f32[2,1,128,1024]{2,0,3,1:T(2,128)} %get-tuple-element.15), channel_id=1, source_target_pairs={{0,4},{1,5},{2,6},{3,7},{4,0},{5,1},{6,2},{7,3},{8,12},{9,13},{10,... | collective-permute-start | bytes 3145736 | tf_op jit(solution)/shard_map/ppermute | solution.py:23
  58.8 65.9 %collective-permute-start.4 = (f32[2,1,128,1024]{2,0,3,1:T(2,128)}, f32[2,1,128,1024]{2,0,3,1:T(2,128)}, u32[]{:S(2)}, u32[]{:S(2)}) collective-permute-start(f32[2,1,128,1024]{2,0,3,1:T(2,128)} %get-tuple-element.16), channel_id=1, source_target_pairs={{0,5},{1,4},{2,7},{3,6},{4,1},{5,0},{6,3},{7,2},{8,13},{9,12},{10,... | collective-permute-start | bytes 3145736 | tf_op jit(solution)/shard_map/ppermute | solution.py:23
  59.0 1.0 copy-start.8
  66.1 5.4 copy-start.6
  66.1 6.4 copy-start.7
  109.5 3.3 copy-start.10
  112.8 27.0 %collective-permute-start.5 = (f32[2,1,128,1024]{2,0,3,1:T(2,128)S(1)}, f32[2,1,128,1024]{2,0,3,1:T(2,128)S(1)}, u32[]{:S(2)}, u32[]{:S(2)}) collective-permute-start(f32[2,1,128,1024]{2,0,3,1:T(2,128)S(1)} %copy-done.10), channel_id=1, source_target_pairs={{0,6},{1,7},{2,4},{3,5},{4,2},{5,3},{6,0},{7,1},{8,14},{9,15},{10,... | collective-permute-start | bytes 3145736 | tf_op jit(solution)/shard_map/ppermute | solution.py:23
  117.8 43.4 %collective-permute-start.6 = (f32[2,1,128,1024]{2,0,3,1:T(2,128)}, f32[2,1,128,1024]{2,0,3,1:T(2,128)S(1)}, u32[]{:S(2)}, u32[]{:S(2)}) collective-permute-start(f32[2,1,128,1024]{2,0,3,1:T(2,128)} %get-tuple-element.11), channel_id=1, source_target_pairs={{0,7},{1,6},{2,5},{3,4},{4,3},{5,2},{6,1},{7,0},{8,15},{9,14},{10,... | collective-permute-start | bytes 3145736 | tf_op jit(solution)/shard_map/ppermute | solution.py:23
  265.5 27.4 %copy-start = (f32[128,64,128]{2,1,0:T(8,128)}, f32[128,64,128]{2,1,0:T(8,128)S(1)}, u32[]{:S(2)}) copy-start(f32[128,64,128]{2,1,0:T(8,128)S(1)} %get-tuple-element.9) | copy-start | bytes 12582916
  265.5 36.9 %copy-start.3 = (f32[128,64,128]{2,1,0:T(8,128)}, f32[128,64,128]{2,1,0:T(8,128)S(1)}, u32[]{:S(2)}) copy-start(f32[128,64,128]{2,1,0:T(8,128)S(1)} %get-tuple-element.10) | copy-start | bytes 12582916
  308.6 325.2 %all-reduce.5.cloned.1.call-start = ((), (), s32[]{:S(2)}) async-start(), calls=%async_computation.1 | async-start | bytes 4194304 | tf_op jit(solution)/shard_map/psum | solution.py:104
  455.1 2.2 copy-start.4
  457.4 11.4 %copy-start.1 = (f32[128,64,128]{2,1,0:T(8,128)S(1)}, f32[128,64,128]{2,1,0:T(8,128)}, u32[]{:S(2)}) copy-start(f32[128,64,128]{2,1,0:T(8,128)} %copy-done) | copy-start | bytes 12582916
  644.1 2.2 copy-start.5
  646.3 11.3 %copy-start.2 = (f32[128,64,128]{2,1,0:T(8,128)S(1)}, f32[128,64,128]{2,1,0:T(8,128)}, u32[]{:S(2)}) copy-start(f32[128,64,128]{2,1,0:T(8,128)} %copy-done) | copy-start | bytes 12582916
Sparse Core Ops, SparseCore 0:
  308.7 136.1 all-reduce.2
  500.4 133.3 all-reduce.4
